TPU v7x, 256 devices: a whole 4x4x8 slice. The times are simulated.
256 devices in a mesh: dp: 8 (over y, z_lo), fsdp: 32 (over z_hi, x, core).
Axes of the slice: x: 4, y: 4, z: 8 (z_hi: 4, z_lo: 2; z = z_hi * 2 + z_lo), core: 2. Of those that a mesh axis runs over, the one named last changes fastest.
Arguments:
- acts: bfloat16 [114688, 7168], P(('dp', 'fsdp')), may hold values from -24 to 24
- upstream: bfloat16 [114688, 512], P(('dp', 'fsdp')), may hold values from -0.4375 to 0.4375
- k_weight: bfloat16 [7168, 512], P('fsdp'), may hold values from -0.0625 to 0.0625
- probe: bfloat16 [7168, 512], P('fsdp'), may hold values from -5 to 5
- norm_gain: float32 [128], replicated, may hold values from 0.1 to 1.9
- momentum: float32 [7168, 512], P('fsdp', 'dp'), may hold values from -4 to 4
- curvature: float32 [7168, 512], P('fsdp', 'dp'), may hold values from 0.3 to 3
Outputs:
- new_momentum: float32 [7168, 512], P('fsdp', 'dp')
- new_curvature: float32 [7168, 512], P('fsdp', 'dp')
- update: float32 [7168, 512], P('fsdp', 'dp')
All inputs are finite; a program needn't handle non-finite values.
Results may differ from a plain program's by a relative error of at most 0.024.
Values may be sent and summed in bfloat16 or wider, within the bound.
A program may use at most 128 MiB of HBM per device.

v0:
```python
import jax
import jax.numpy as jnp
from jax import lax
from jax.sharding import PartitionSpec as P


def head_terms(projected, tangent, upstream, norm_gain):
    token_count = projected.shape[0]
    head_size = norm_gain.shape[0]
    head_count = projected.shape[1] // head_size
    shaped = (token_count, head_count, head_size)
    values = projected.reshape(shaped)
    moving = tangent.reshape(shaped)
    weighted = upstream.astype(jnp.float32).reshape(shaped) * norm_gain
    inverse = lax.rsqrt(jnp.mean(values * values, axis=-1, keepdims=True) + 1e-06)
    cubed = inverse * inverse * inverse
    along = jnp.sum(weighted * values, axis=-1, keepdims=True)
    grad_vals = inverse * weighted - cubed * values * along / head_size
    inverse_dot = -cubed * jnp.sum(values * moving, axis=-1, keepdims=True) / head_size
    along_dot = jnp.sum(weighted * moving, axis=-1, keepdims=True)
    hvp_vals = (
        inverse_dot * weighted
        - (
            3.0 * inverse * inverse * inverse_dot * values * along
            + cubed * moving * along
            + cubed * values * along_dot
        )
        / head_size
    )
    return (grad_vals.reshape(token_count, -1), hvp_vals.reshape(token_count, -1))


def contract_tokens(left, right):
    return lax.dot_general(
        left, right, (((0,), (0,)), ((), ())), preferred_element_type=jnp.float32
    )


def on_device(acts, upstream, k_weight, probe, norm_gain, momentum, curvature):
    width = k_weight.shape[1]
    weight_piece = lax.all_gather(k_weight, "fsdp", axis=0, tiled=True)
    probe_piece = lax.all_gather(probe, "fsdp", axis=0, tiled=True)
    projected = jnp.dot(acts, weight_piece, preferred_element_type=jnp.float32)
    tangent = jnp.dot(acts, probe_piece, preferred_element_type=jnp.float32)
    grad_vals, hvp_vals = head_terms(projected, tangent, upstream, norm_gain)
    stacked = jnp.concatenate([grad_vals, hvp_vals], axis=1).astype(jnp.bfloat16)
    owned = lax.psum_scatter(
        contract_tokens(acts, stacked).astype(jnp.bfloat16), "fsdp", scatter_dimension=0, tiled=True
    ).astype(jnp.float32)
    grad_owned = owned[:, :width]
    hvp_owned = owned[:, width:]
    grad_share, hvp_share = (
        lax.psum_scatter(grad_owned, "dp", scatter_dimension=1, tiled=True),
        lax.psum_scatter(hvp_owned, "dp", scatter_dimension=1, tiled=True),
    )
    share_width = grad_share.shape[1]
    probe_cols = lax.dynamic_slice_in_dim(
        probe, lax.axis_index("dp") * share_width, share_width, 1
    ).astype(jnp.float32)
    new_momentum = 0.965 * momentum + 0.035 * grad_share
    new_curvature = 0.99 * curvature + 0.01 * (probe_cols * hvp_share)
    update = jnp.clip(new_momentum / jnp.maximum(0.5 * new_curvature, 0.25), -1.0, 1.0)
    return (new_momentum, new_curvature, update)


def solution(mesh):
    return jax.shard_map(
        on_device,
        mesh=mesh,
        in_specs=(
            P(("dp", "fsdp"), None),
            P(("dp", "fsdp"), None),
            P("fsdp", None),
            P("fsdp", None),
            P(),
            P("fsdp", "dp"),
            P("fsdp", "dp"),
        ),
        out_specs=(P("fsdp", "dp"), P("fsdp", "dp"), P("fsdp", "dp")),
        check_vma=False,
    )
```

profile of v0, /device:TPU:8, one launch (start us, length us, event | category | flops | bytes accessed | tf_op | source)
XLA Modules:
  0.0 463.5 jit_solution(4802881140647189085)
XLA Ops:
  7.2 0.0 all-gather.3.cloned.1.call-start
  7.2 0.7 all-gather.3.cloned.1.call-update
  7.9 0.0 all-gather.5.cloned.1.call-start
  7.9 0.7 all-gather.5.cloned.1.call-update
  8.6 0.0 reduce-scatter.10.cloned.1.call-start
  8.7 1.3 reshape.67
  10.0 0.7 broadcast_bitcast_fusion
  10.7 75.3 %all-gather.3.cloned.1.call-done = bf16[7168,512]{1,0:T(8,128)(2,1)} async-done(((bf16[224,512]{1,0:T(8,128)(2,1)}), bf16[7168,512]{1,0:T(8,128)(2,1)}) %all-gather.3.cloned.1.call-update) | async-done | bytes 7340048 | tf_op jit(solution)/shard_map/all_gather | solution.py:41
  85.9 7.7 %fusion.23 = f32[448,512]{1,0:T(8,128)S(1)} fusion(bf16[448,7168]{1,0:T(8,128)(2,1)} %param.7, bf16[7168,512]{1,0:T(8,128)(2,1)} %all-gather.3.cloned.1.call-done), kind=kOutput, calls=%fused_computation.44 | convolution fusion | flops 3288334336 | bytes 14680064 | tf_op jit(solution)/shard_map/dot_general | solution.py:43
  93.6 0.3 reshape.66
  93.9 0.0 copy-start.7
  94.0 66.8 %all-gather.5.cloned.1.call-done = bf16[7168,512]{1,0:T(8,128)(2,1)} async-done(((bf16[224,512]{1,0:T(8,128)(2,1)}), bf16[7168,512]{1,0:T(8,128)(2,1)}) %all-gather.5.cloned.1.call-update) | async-done | bytes 7340048 | tf_op jit(solution)/shard_map/all_gather | solution.py:42
  160.8 0.0 copy-done
  160.8 9.4 %fusion.24 = f32[448,512]{1,0:T(8,128)} fusion(bf16[448,7168]{1,0:T(8,128)(2,1)} %param.7, bf16[7168,512]{1,0:T(8,128)(2,1)} %all-gather.5.cloned.1.call-done), kind=kOutput, calls=%fused_computation.45 | convolution fusion | flops 3288334336 | bytes 14680064 | tf_op jit(solution)/shard_map/dot_general | solution.py:44
  170.1 1.5 reshape.68
  171.6 0.0 copy-start.4
  171.6 1.6 multiply_reduce_fusion.3
  173.2 1.5 fusion
  174.8 1.5 fusion.1
  176.3 1.2 copy.17
  177.4 0.1 copy.20
  177.6 0.1 copy.22
  177.7 0.9 copy.18
  178.6 0.8 copy.19
  179.4 0.8 copy.21
  180.2 0.5 mul.254
  180.8 1.7 mul.227
  182.5 1.5 mul.236
  184.0 1.5 mul.247
  185.5 0.0 slice-start.1
  185.5 2.3 fusion.10
  187.8 0.0 slice-done
  187.9 0.0 slice-done.1
  187.9 11.3 %convert_bitcast_fusion = bf16[7168,1024]{0,1:T(8,128)(2,1)} fusion(bf16[448,7168]{1,0:T(8,128)(2,1)S(1)} %bitcast.67, bf16[448,512]{1,0:T(8,128)(2,1)S(1)} %get-tuple-element.9, bf16[448,512]{1,0:T(8,128)(2,1)S(1)} %get-tuple-element.8), kind=kOutput, calls=%fused_computation.2 | convolution fusion | flops 6585843712 | bytes 22020096 | tf_op jit(solution)/shard_map/dot_general | solution.py:34
  199.2 19.9 %copy.24 = bf16[7168,1024]{1,0:T(8,128)(2,1)} copy(bf16[7168,1024]{0,1:T(8,128)(2,1)} %convert_bitcast_fusion) | data formatting | bytes 29360128
  219.1 0.0 reduce-scatter.10.cloned.1.call-update
  219.1 0.0 reduce-scatter.6.cloned.1.call-start
  219.2 153.2 %reduce-scatter.10.cloned.1.call-done = bf16[224,1024]{1,0:T(8,128)(2,1)} async-done(((bf16[7168,1024]{1,0:T(8,128)(2,1)}), bf16[224,1024]{1,0:T(8,128)(2,1)}) %reduce-scatter.10.cloned.1.call-update) | async-done | bytes 458768
  372.4 1.2 copy.25
  373.6 1.0 fusion.22
  374.6 0.0 reduce-scatter.6.cloned.1.call-update
  374.6 0.0 reduce-scatter.8.cloned.1.call-start
  374.7 0.5 reduce-scatter.8.cloned.1.call-update
  375.2 0.9 constant_dynamic-slice_fusion
  376.2 0.1 copy.26
  376.2 37.5 %reduce-scatter.6.cloned.1.call-done = f32[224,64]{0,1:T(8,128)} async-done(((f32[224,512]{0,1:T(8,128)}), f32[224,64]{0,1:T(8,128)}) %reduce-scatter.6.cloned.1.call-update) | async-done | bytes 57360 | tf_op jit(solution)/shard_map/reduce_scatter | solution.py:53
  413.7 41.7 %reduce-scatter.8.cloned.1.call-done = f32[224,64]{0,1:T(8,128)} async-done(((f32[224,512]{0,1:T(8,128)}), f32[224,64]{0,1:T(8,128)}) %reduce-scatter.8.cloned.1.call-update) | async-done | bytes 57360 | tf_op jit(solution)/shard_map/reduce_scatter | solution.py:54
  455.5 1.6 divide_clamp_fusion
  (16 shorter events, 0.1 us)
Async XLA Ops:
  7.2 78.8 %all-gather.3.cloned.1.call-start = ((), (), s32[]{:S(2)}) async-start(), calls=%async_computation.3 | async-start | bytes 7569408 | tf_op jit(solution)/shard_map/all_gather | solution.py:41
  7.9 152.9 %all-gather.5.cloned.1.call-start = ((), (), s32[]{:S(2)}) async-start(), calls=%async_computation.4 | async-start | bytes 7569408 | tf_op jit(solution)/shard_map/all_gather | solution.py:42
  8.6 363.7 %reduce-scatter.10.cloned.1.call-start = ((), (), s32[]{:S(2)}) async-start(), calls=%async_computation.7 | async-start | bytes 15138816
  93.6 67.1 %copy-start = (f32[448,512]{1,0:T(8,128)}, f32[448,512]{1,0:T(8,128)S(1)}, u32[]{:S(2)}) copy-start(f32[448,512]{1,0:T(8,128)S(1)} %fusion.23) | copy-start | bytes 2752516
  93.9 79.3 %copy-start.7 = (f32[128]{0:T(128)S(1)}, f32[128]{0:T(128)}, u32[]{:S(2)}) copy-start(f32[128]{0:T(128)} %param.11) | copy-start | bytes 1540
  171.6 13.9 %copy-start.4 = (bf16[448,512]{1,0:T(8,128)(2,1)S(1)}, bf16[448,512]{1,0:T(8,128)(2,1)}, u32[]{:S(2)}) copy-start(bf16[448,512]{1,0:T(8,128)(2,1)} %param.8) | copy-start | bytes 1376260
  174.8 10.7 %copy-start.1 = (f32[448,512]{1,0:T(8,128)S(1)}, f32[448,512]{1,0:T(8,128)}, u32[]{:S(2)}) copy-start(f32[448,512]{1,0:T(8,128)} %copy-done) | copy-start | bytes 2752516
  176.2 9.3 %copy-start.2 = (f32[448,512]{1,0:T(8,128)S(1)}, f32[448,512]{1,0:T(8,128)}, u32[]{:S(2)}) copy-start(f32[448,512]{1,0:T(8,128)} %fusion.24) | copy-start | bytes 2752516
  176.2 9.3 %copy-start.3 = (f32[448,4,128]{2,1,0:T(4,128)S(1)}, f32[448,4,128]{2,1,0:T(4,128)}, u32[]{:S(2)}) copy-start(f32[448,4,128]{2,1,0:T(4,128)} %fusion) | copy-start | bytes 2752516
  180.2 7.6 %slice-start = ((s8[6422528]{0:T(1024)(128)(4,1)}), s8[4194304]{0:T(1024)(128)(4,1)S(1)}, s32[]{:S(2)}) async-start(s8[6422528]{0:T(1024)(128)(4,1)} %bitcast.66), calls=%async_computation.8 | async-start | bytes 8388608
  185.5 2.3 slice-start.1
  219.1 236.3 %copy-start.5 = (f32[224,64]{0,1:T(8,128)S(1)}, f32[224,64]{0,1:T(8,128)}, u32[]{:S(2)}) copy-start(f32[224,64]{0,1:T(8,128)} %param.13) | copy-start | bytes 172036
  219.1 236.3 %copy-start.6 = (f32[224,64]{0,1:T(8,128)S(1)}, f32[224,64]{0,1:T(8,128)}, u32[]{:S(2)}) copy-start(f32[224,64]{0,1:T(8,128)} %param.12) | copy-start | bytes 172036
  219.1 194.6 %reduce-scatter.6.cloned.1.call-start = ((), (), s32[]{:S(2)}) async-start(), calls=%async_computation.5 | async-start | bytes 589824 | tf_op jit(solution)/shard_map/reduce_scatter | solution.py:53
  374.6 80.8 %reduce-scatter.8.cloned.1.call-start = ((), (), s32[]{:S(2)}) async-start(), calls=%async_computation.6 | async-start | bytes 589824 | tf_op jit(solution)/shard_map/reduce_scatter | solution.py:54
Sparse Core Ops, SparseCore 0:
  10.5 75.3 all-gather.2
  88.5 72.2 all-gather.4
  219.3 153.0 reduce-scatter.9
  374.8 38.9 reduce-scatter.5
  416.1 39.3 reduce-scatter.7
where the time goes:
time: 467 us; the launch traced here: 464 us
  waiting for transfers between devices  376 us (81%)
  local copies, waits for them, and re-layouts  36.1 us (8%)
  matrix products  28.4 us (6%)
  between operations  13.9 us (3%)
  other arithmetic  8.53 us (2%)
    unnamed x6, waiting for transfers between devices  155 us
    all_gather x1, waiting for transfers between devices, on_device(): weight_piece = lax.all_gather(k_weight, 'fsdp', axis=0, tiled=True)  75.3 us
    all_gather x1, waiting for transfers between devices, on_device(): probe_piece = lax.all_gather(probe, 'fsdp', axis=0, tiled=True)  66.8 us
    reduce_scatter x1, waiting for transfers between devices, on_device(): lax.psum_scatter(hvp_owned, 'dp', scatter_dimension=1, tiled=True)  41.7 us
    reduce_scatter x1, waiting for transfers between devices, on_device(): lax.psum_scatter(grad_owned, 'dp', scatter_dimension=1, tiled=True)  37.5 us
    unnamed x23, local copies, waits for them, and re-layouts  21.3 us
    dot_general x1, matrix products, contract_tokens(): lax.dot_general(left, right, (((0,), (0,)), ((), ())), preferred_element_...  11.3 us
    dot_general x1, matrix products, on_device(): tangent = jnp.dot(acts, probe_piece, preferred_element_type=jnp.float32)  9.37 us
  transfers between devices with their start and end apart: 5, of which 5 were waited for; matrix products, arithmetic and copies ran while one was open for 2% of the time, Pallas kernels for 0%

commit v1 on v0

v1 whole, which is shorter than its diff:
```python
import jax
import jax.numpy as jnp
from jax import lax
from jax.experimental import pallas as pl
from jax.experimental.pallas import tpu as pltpu
from jax.sharding import PartitionSpec as P

MESH = pl.DeviceIdType.MESH
F32 = jnp.float32
BF16 = jnp.bfloat16
TOK = 448
D = 7168
NX = 400


def kernel(acts, upstream, k_weight, probe, gain, momentum, curvature,
           out_m, out_c, out_u,
           wp, av, at, acc, upv, gs, csend, crecv, rsend, rech, recf, s_buf,
           yrecv, t_buf, zrecv, mom_v, cur_v, send_sems, recv_sems, loc_sems):
    dp = lax.axis_index("dp")
    fs = lax.axis_index("fsdp")
    y, zl = dp // 2, lax.rem(dp, 2)
    zh, x, c = fs // 8, lax.rem(fs // 2, 4), lax.rem(fs, 2)

    def m4(v):
        return lax.rem(v + 8, 4)

    def dev(dx=0, dy=0, dz=0):
        return (m4(y + dy) * 2 + zl, m4(zh + dz) * 8 + m4(x + dx) * 2 + c)

    def dev_z(z):
        return (y * 2 + lax.rem(z, 2), (z // 2) * 8 + x * 2 + c)

    partner = (dp, zh * 8 + x * 2 + (1 - c))
    z = 2 * zh + zl

    barrier = pltpu.get_barrier_semaphore()
    peers = [partner]
    for d in (1, 2, 3):
        peers += [dev(dx=d), dev(dy=d)]
    for d in range(1, 8):
        peers.append(dev_z(lax.rem(z + d, 8)))

    def local(src, dst, i):
        cp = pltpu.make_async_copy(src, dst, loc_sems.at[i])
        cp.start()
        return cp

    low_rows, high_rows = pl.ds(0, 112), pl.ds(112, 112)
    quarter = wp.at[zh, x, c, high_rows, pl.ds(pl.multiple_of(y * 256, 256), 256)]
    part_cols = pl.ds(pl.multiple_of(lax.rem(y, 2) * 256, 256), 256)

    @pl.when(y < 2)
    def _():
        pltpu.make_async_copy(k_weight.at[high_rows, part_cols], quarter, loc_sems.at[13]).start()

    @pl.when(y >= 2)
    def _():
        pltpu.make_async_copy(probe.at[high_rows, part_cols], quarter, loc_sems.at[13]).start()

    own = [local(k_weight.at[low_rows], wp.at[zh, x, c, low_rows, pl.ds(0, 512)], 0),
           local(probe.at[low_rows], wp.at[zh, x, c, low_rows, pl.ds(512, 512)], 1),
           pltpu.make_async_copy(k_weight.at[high_rows, part_cols], quarter, loc_sems.at[13])]
    acp = [local(acts.at[:, pl.ds(i * 896, 896)], av.at[:, pl.ds(i * 896, 896)], 2 + i) for i in range(8)]
    misc = [local(upstream, upv, 10), local(momentum, mom_v, 11), local(curvature, cur_v, 12)]

    for p in peers:
        pl.semaphore_signal(barrier, inc=1, device_id=p, device_id_type=MESH)
    pl.semaphore_wait(barrier, len(peers))

    count = [0]
    sent = []

    def take(n):
        base = count[0]
        count[0] += n
        return base

    def rdma(src, dst, device, i):
        return pltpu.make_async_remote_copy(
            src_ref=src, dst_ref=dst, send_sem=send_sems.at[i], recv_sem=recv_sems.at[i],
            device_id=device, device_id_type=MESH)

    def xfer(src, dst, device):
        cp = rdma(src, dst, device, take(1))
        cp.start()
        sent.append(cp)
        return cp

    class Ring:
        def __init__(self, region, half, coord, up, down):
            self.region, self.half, self.coord, self.up, self.down = region, half, coord, up, down

        def start(self):
            r = self.region(self.coord)
            self.p = xfer(r, r, self.up)
            self.m = xfer(r, r, self.down)

        def mid(self):
            self.p.wait_recv()
            r = self.half(m4(self.coord - 1), 0)
            self.hp = xfer(r, r, self.up)
            self.m.wait_recv()
            r = self.half(m4(self.coord + 1), 1)
            self.hm = xfer(r, r, self.down)

        def end(self):
            self.hp.wait_recv()
            self.hm.wait_recv()

    lo, hi = pl.ds(0, 112), pl.ds(112, 112)
    yc = pl.multiple_of(y * 256, 256)

    def bz_half(q, i):
        return wp.at[q, x, c, hi, pl.ds(pl.multiple_of(yc + i * 128, 128), 128)]

    bz = Ring(lambda q: wp.at[q, x, c, hi, pl.ds(yc, 256)], bz_half, zh, dev(dz=1), dev(dz=-1))
    az = Ring(lambda q: wp.at[q, x, c, lo, :],
              lambda q, i: wp.at[q, x, c, lo, pl.ds(i * 512, 512)], zh, dev(dz=1), dev(dz=-1))
    bx, ax, by = {}, {}, {}
    for dz in (0, -1, 1, 2):
        def mk(q):
            bx[dz] = Ring(lambda k: wp.at[q, k, c, hi, pl.ds(yc, 256)],
                          lambda k, i: wp.at[q, k, c, hi, pl.ds(pl.multiple_of(yc + i * 128, 128), 128)],
                          x, dev(dx=1), dev(dx=-1))
            ax[dz] = Ring(lambda k: wp.at[q, k, c, lo, :],
                          lambda k, i: wp.at[q, k, c, lo, pl.ds(i * 512, 512)],
                          x, dev(dx=1), dev(dx=-1))
            by[dz] = Ring(lambda k: wp.at[q, :, c, hi, pl.ds(pl.multiple_of(k * 256, 256), 256)],
                          lambda k, i: wp.at[q, pl.ds(2 * i, 2), c, hi, pl.ds(pl.multiple_of(k * 256, 256), 256)],
                          y, dev(dy=1), dev(dy=-1))
        mk(m4(zh + dz))

    core = {}

    def core_send(kind, dz):
        r = wp.at[m4(zh + dz), :, c, lo if kind == "a" else hi, :]
        core[kind, dz] = xfer(r, r, partner)

    def transpose(i):
        acp[i].wait()
        q, xp = i // 2, i % 2
        blk = av[:, i * 896:(i + 1) * 896]
        tr = blk.T
        for xx in range(2):
            for cc in range(2):
                for col in range(2):
                    r0 = xx * 448 + cc * 224 + col * 112
                    at[col, xp * 2 + xx, cc, pl.ds(q * 112, 112), :] = tr[r0:r0 + 112, :]

    first = [True]

    def forward(dz):
        core["a", dz].wait_recv()
        core["b", dz].wait_recv()
        q = m4(zh + dz)
        init = first[0]
        first[0] = False
        for n in range(2):
            total = None if init else acc[:, n * 512:(n + 1) * 512]
            for xp in range(2):
                lhs = av[:, pl.ds(pl.multiple_of(q * 1792 + xp * 896, 128), 896)]
                rhs = wp[q, xp * 2:xp * 2 + 2, :, :, n * 512:(n + 1) * 512].reshape(896, 512)
                part = jnp.dot(lhs, rhs, preferred_element_type=F32)
                total = part if total is None else total + part
            acc[:, n * 512:(n + 1) * 512] = total

    for cp in own:
        cp.wait()
    bz.start()
    bx[0].start()
    ax[0].start()
    transpose(0)
    bx[0].mid()
    bz.mid()
    az.start()
    bx[-1].start()
    bx[1].start()
    transpose(1)
    bx[0].end()
    by[0].start()
    transpose(2)
    bx[-1].mid()
    bx[1].mid()
    ax[0].mid()
    bz.end()
    bx[2].start()
    transpose(3)
    bx[-1].end()
    by[-1].start()
    bx[1].end()
    by[1].start()
    transpose(4)
    bx[2].mid()
    transpose(5)
    bx[2].end()
    by[2].start()
    by[0].mid()
    ax[0].end()
    core_send("a", 0)
    transpose(6)
    az.mid()
    ax[-1].start()
    ax[1].start()
    transpose(7)
    by[0].end()
    core_send("b", 0)
    by[-1].mid()
    forward(0)
    az.end()
    ax[2].start()
    by[-1].end()
    core_send("b", -1)
    ax[-1].mid()
    ax[1].mid()
    by[1].mid()
    ax[-1].end()
    core_send("a", -1)
    by[1].end()
    core_send("b", 1)
    forward(-1)
    ax[1].end()
    core_send("a", 1)
    by[2].mid()
    ax[2].mid()
    forward(1)
    by[2].end()
    core_send("b", 2)
    ax[2].end()
    core_send("a", 2)
    for cp in misc:
        cp.wait()
    forward(2)

    RB = 64

    def head(i, carry):
        h, rb = i // 7, lax.rem(i, 7)
        rows = pl.ds(pl.multiple_of(rb * RB, RB), RB)
        cols = pl.ds(pl.multiple_of(h * 128, 128), 128)
        yv = acc[rows, cols]
        tv = acc[rows, pl.ds(pl.multiple_of(512 + h * 128, 128), 128)]
        w = upv[rows, cols].astype(F32) * gain[...]
        inv = lax.rsqrt(jnp.sum(yv * yv, axis=-1, keepdims=True) * (1.0 / 128) + 1e-06)
        cubed = inv * inv * inv
        along = jnp.sum(w * yv, axis=-1, keepdims=True)
        yt = jnp.sum(yv * tv, axis=-1, keepdims=True)
        along_dot = jnp.sum(w * tv, axis=-1, keepdims=True)
        k1 = cubed * along * (1.0 / 128)
        inv_dot = -cubed * yt * (1.0 / 128)
        k2 = (3.0 * inv * inv * inv_dot * along + cubed * along_dot) * (1.0 / 128)
        g = inv * w - yv * k1
        hv = inv_dot * w - (yv * k2 + tv * k1)
        low = lax.broadcasted_iota(jnp.int32, (RB, 128), 1) < 64
        gr = pltpu.roll(g, 64, axis=1)
        hr = pltpu.roll(hv, 64, axis=1)
        gs[h, rows, pl.ds(0, 128)] = jnp.where(low, g, hr).astype(BF16)
        gs[h, rows, pl.ds(128, 128)] = jnp.where(low, gr, hv).astype(BF16)
        return carry

    lax.fori_loop(0, 28, head, 0)

    u = (x, y)
    v_own = (y, x)

    def udev(k, d):
        return dev(dx=d) if k == 0 else dev(dy=d)

    def vdev(k, d):
        return dev(dy=d) if k == 0 else dev(dx=d)

    def tile(k, uq, v, cc):
        xi, yj = (uq, v) if k == 0 else (v, uq)
        return jnp.dot(at[k, xi, cc], gs[yj], preferred_element_type=F32)

    ds_order = (2, 1, -1, 0)
    core_rs = {}

    def part_p(k, i):
        if i >= 2:
            core_rs[k, i - 2].wait_send()
            sent[:] = [cp for cp in sent if cp is not core_rs[k, i - 2]]
        uq = m4(u[k] + ds_order[i])

        def body(v, carry):
            csend[k, i % 2, v] = tile(k, uq, v, 1 - c).astype(BF16)
            return carry

        lax.fori_loop(0, 4, body, 0)
        core_rs[k, i] = xfer(csend.at[k, i % 2], crecv.at[k, i], partner)

    half_base = {}

    def half_copy(k, v):
        device = udev(k, 1 - 2 * (v // 2))
        return rdma(rsend.at[k, 0, v], rech.at[k, v], device, half_base[k] + v)

    def part_far(k):
        core_rs[k, 0].wait_recv()
        half_base[k] = take(4)
        uq = m4(u[k] + 2)

        def body(v, carry):
            rsend[k, 0, v] = (tile(k, uq, v, c) + crecv[k, 0, v].astype(F32)).astype(BF16)
            half_copy(k, v).start()
            return carry

        lax.fori_loop(0, 4, body, 0)

    early, late = {}, {}
    zorder = (2, 1, -1, 0)

    def near_free(k, i):
        core_rs[k, i].wait_recv()
        d = ds_order[i]
        uq = m4(u[k] + d)
        v0 = 2 if d == 1 else 0

        def body(v, carry):
            rsend[k, i, v] = (tile(k, uq, v, c) + crecv[k, i, v].astype(F32)).astype(BF16)
            return carry

        lax.fori_loop(v0, v0 + 2, body, 0)
        early[k, i] = xfer(rsend.at[k, i, pl.ds(v0, 2)], recf.at[k, i - 1, pl.ds(v0, 2)], udev(k, d))

    def near_sum(k, i):
        d = ds_order[i]
        uq = m4(u[k] + d)
        v0 = 0 if d == 1 else 2
        half_copy(k, v0).wait_recv()
        half_copy(k, v0 + 1).wait_recv()

        def body(v, carry):
            rsend[k, i, v] = (tile(k, uq, v, c) + crecv[k, i, v].astype(F32) + rech[k, v].astype(F32)).astype(BF16)
            return carry

        lax.fori_loop(v0, v0 + 2, body, 0)
        for dz in zorder:
            rows = pl.ds(pl.multiple_of(m4(zh + dz) * 112, 16), 112)
            late[k, i, dz] = xfer(rsend.at[k, i, pl.ds(v0, 2), rows], recf.at[k, i - 1, pl.ds(v0, 2), rows], udev(k, d))

    def part_own(k):
        core_rs[k, 3].wait_recv()

        def body(v, carry):
            s_buf[k, v] = (tile(k, u[k], v, c) + crecv[k, 3, v].astype(F32)).astype(BF16)
            return carry

        lax.fori_loop(0, 4, body, 0)

    phase2 = {}

    def chunk_sum(k, dz):
        rows = pl.ds(pl.multiple_of(m4(zh + dz) * 112, 16), 112)
        for i in (1, 2):
            if dz == zorder[0]:
                early[k, i].wait_recv()
            late[k, i, dz].wait_recv()

        def body(v, carry):
            s_buf[k, v, rows] = (s_buf[k, v, rows].astype(F32) + recf[k, 0, v, rows].astype(F32)
                                 + recf[k, 1, v, rows].astype(F32)).astype(BF16)
            return carry

        lax.fori_loop(0, 4, body, 0)
        for d in (2, 1, 3):
            vq = m4(v_own[k] + d)
            phase2[k, dz, d] = xfer(s_buf.at[k, vq, rows], yrecv.at[k, d - 1, rows], vdev(k, d))

    zbase = (take(8), take(8))

    def z_copy(k, rows, target, cols):
        delta = lax.rem(z - target + 8, 8)
        return rdma(t_buf.at[k, rows, pl.ds(pl.multiple_of(cols * 128, 128), 128)],
                    zrecv.at[k, delta], dev_z(target), zbase[k] + delta)

    def chunk_z(k, dz):
        q = m4(zh + dz)
        rows = pl.ds(pl.multiple_of(q * 112, 16), 112)
        for d in (1, 2, 3):
            phase2[k, dz, d].wait_recv()
        total = s_buf[k, v_own[k], rows].astype(F32)
        for d in range(3):
            total = total + yrecv[k, d, rows].astype(F32)
        t_buf[k, rows] = total.astype(BF16)
        if dz == 0:
            z_copy(k, rows, 2 * zh + (1 - zl), 1 - zl).start()
        else:
            for l in range(2):
                z_copy(k, rows, 2 * q + l, jnp.int32(l)).start()

    part_p(0, 0)
    part_p(1, 0)
    part_far(0)
    part_far(1)
    part_p(0, 1)
    part_p(0, 2)
    part_p(1, 1)
    part_p(1, 2)
    near_free(0, 1)
    near_free(0, 2)
    near_free(1, 1)
    near_free(1, 2)
    part_p(0, 3)
    part_p(1, 3)
    near_sum(0, 1)
    near_sum(0, 2)
    near_sum(1, 1)
    near_sum(1, 2)
    part_own(0)
    part_own(1)
    for j, dz in enumerate(zorder):
        for k in range(2):
            chunk_sum(k, dz)
            if j:
                chunk_z(k, zorder[j - 1])
    for k in range(2):
        chunk_z(k, zorder[-1])

    own_rows = pl.ds(pl.multiple_of(zh * 112, 16), 112)
    for k in range(2):
        for d in range(1, 8):
            pltpu.make_async_remote_copy(
                src_ref=zrecv.at[k, 0], dst_ref=zrecv.at[k, d], send_sem=send_sems.at[zbase[k] + d],
                recv_sem=recv_sems.at[zbase[k] + d], device_id=partner, device_id_type=MESH).wait_recv()
        total = t_buf[k, own_rows, pl.ds(pl.multiple_of(zl * 128, 128), 128)].astype(F32)
        for d in range(1, 8):
            total = total + zrecv[k, d].astype(F32)
        rk = pl.ds(k * 112, 112)
        g = total[:, :64]
        hv = pltpu.roll(total, 64, axis=1)[:, :64]
        pc = wp[zh, x, c, rk, pl.ds(pl.multiple_of(512 + y * 128, 128), 128)].astype(F32)
        pcr = pltpu.roll(pc, 64, axis=1)
        pv = jnp.where(zl == 0, pc, pcr)[:, :64]
        nm = 0.965 * mom_v[rk, :] + 0.035 * g
        nc = 0.99 * cur_v[rk, :] + 0.01 * (pv * hv)
        out_m[rk, :] = nm
        out_c[rk, :] = nc
        out_u[rk, :] = jnp.clip(nm / jnp.maximum(0.5 * nc, 0.25), -1.0, 1.0)

    for cp in sent:
        cp.wait_send()
    for k in range(2):
        for v in range(4):
            half_copy(k, v).wait_send()
        for d in range(1, 8):
            pltpu.make_async_remote_copy(
                src_ref=zrecv.at[k, 0], dst_ref=zrecv.at[k, d], send_sem=send_sems.at[zbase[k] + d],
                recv_sem=recv_sems.at[zbase[k] + d], device_id=partner, device_id_type=MESH).wait_send()
    assert count[0] <= NX, count[0]


def on_device(acts, upstream, k_weight, probe, norm_gain, momentum, curvature):
    any_spec = pl.BlockSpec(memory_space=pl.ANY)
    vmem = pl.BlockSpec(memory_space=pltpu.VMEM)
    out = jax.ShapeDtypeStruct((224, 64), F32)
    return pl.pallas_call(
        kernel,
        out_shape=(out, out, out),
        in_specs=[any_spec] * 4 + [vmem] + [any_spec] * 2,
        out_specs=(vmem, vmem, vmem),
        scratch_shapes=[
            pltpu.VMEM((4, 4, 2, 224, 1024), BF16),
            pltpu.VMEM((TOK, D), BF16),
            pltpu.VMEM((2, 4, 2, 448, 448), BF16),
            pltpu.VMEM((TOK, 1024), F32),
            pltpu.VMEM((TOK, 512), BF16),
            pltpu.VMEM((4, TOK, 256), BF16),
            pltpu.VMEM((2, 2, 4, 448, 256), BF16),
            pltpu.VMEM((2, 4, 4, 448, 256), BF16),
            pltpu.VMEM((2, 3, 4, 448, 256), BF16),
            pltpu.VMEM((2, 4, 448, 256), BF16),
            pltpu.VMEM((2, 2, 4, 448, 256), BF16),
            pltpu.VMEM((2, 4, 448, 256), BF16),
            pltpu.VMEM((2, 3, 448, 256), BF16),
            pltpu.VMEM((2, 448, 256), BF16),
            pltpu.VMEM((2, 8, 112, 128), BF16),
            pltpu.VMEM((224, 64), F32),
            pltpu.VMEM((224, 64), F32),
            pltpu.SemaphoreType.DMA((NX,)),
            pltpu.SemaphoreType.DMA((NX,)),
            pltpu.SemaphoreType.DMA((16,)),
        ],
        compiler_params=pltpu.CompilerParams(
            collective_id=0, has_side_effects=True, vmem_limit_bytes=67043328),
    )(acts, upstream, k_weight, probe, norm_gain.reshape(1, 128), momentum, curvature)


def solution(mesh):
    return jax.shard_map(
        on_device,
        mesh=mesh,
        in_specs=(
            P(("dp", "fsdp"), None),
            P(("dp", "fsdp"), None),
            P("fsdp", None),
            P("fsdp", None),
            P(),
            P("fsdp", "dp"),
            P("fsdp", "dp"),
        ),
        out_specs=(P("fsdp", "dp"), P("fsdp", "dp"), P("fsdp", "dp")),
        check_vma=False,
    )
```

time: 467 us -> 147 us (0.31)
  waiting for transfers between devices: 376 us -> 0 us
  Pallas kernels: 0 us -> 138 us
  matrix products: 28.4 us -> 0 us
  local copies, waits for them, and re-layouts: 36.1 us -> 7.98 us
  between operations: 13.9 us -> 0.64 us
  other arithmetic: 8.53 us -> 0 us
    unnamed x6 -> x0, waiting for transfers between devices: 155 us -> none
    all_gather x2 -> x0, waiting for transfers between devices: 142 us -> none  [the longest x1 75.3 us: on_device(): weight_piece = lax.all_gather(k_weight, 'fsdp', axis=0, tiled=True)]
    pallas_call x0 -> x1, Pallas kernels: none -> 138 us  [on_device(): pl.pallas_call(kernel, out_shape=(out, out, out), in_specs=[any_spec] * 4...]
    reduce_scatter x2 -> x0, waiting for transfers between devices: 79.2 us -> none  [the longest x1 41.7 us: on_device(): lax.psum_scatter(hvp_owned, 'dp', scatter_dimension=1, tiled=True)]
    dot_general x3 -> x0, matrix products: 28.4 us -> none  [the longest x1 11.3 us: contract_tokens(): lax.dot_general(left, right, (((0,), (0,)), ((), ())), preferred_element_...]
    unnamed x23 -> x2, local copies, waits for them, and re-layouts: 21.3 us -> 3.15 us
    mul x7 -> x0, local copies, waits for them, and re-layouts: 6.84 us -> none  [the longest x2 3.21 us: head_terms(): grad_vals = inverse * weighted - cubed * values * along / head_size]
    pallas_call x0 -> x3, local copies, waits for them, and re-layouts: none -> 4.83 us  [on_device(): pl.pallas_call(kernel, out_shape=(out, out, out), in_specs=[any_spec] * 4...]
  transfers between devices with their start and end apart: 5 -> 0, of which waited for: 5 -> 0; matrix products, arithmetic and copies ran while one was open for 2% -> 0% of each run, Pallas kernels for 0% -> 0%
where the time goes in v1:
time: 147 us
  Pallas kernels  138 us (94%)
  local copies, waits for them, and re-layouts  7.98 us (5%)
    pallas_call x1, Pallas kernels, on_device(): pl.pallas_call(kernel, out_shape=(out, out, out), in_specs=[any_spec] * 4...  138 us
    pallas_call x3, local copies, waits for them, and re-layouts, on_device(): pl.pallas_call(kernel, out_shape=(out, out, out), in_specs=[any_spec] * 4...  4.83 us
    unnamed x2, local copies, waits for them, and re-layouts  3.15 us

profile of v1, /device:TPU:8, one launch (start us, length us, event | category | flops | bytes accessed | tf_op | source)
XLA Modules:
  0.0 146.8 jit_solution(10633623007337710846)
XLA Ops:
  0.6 1.6 %copy.10.momentum = f32[224,64]{1,0:T(8,128)} copy(f32[224,64]{0,1:T(8,128)} %param.12) | data formatting | bytes 114688 | tf_op args[5]
  2.2 1.6 %copy.11.curvature = f32[224,64]{1,0:T(8,128)} copy(f32[224,64]{0,1:T(8,128)} %param.13) | data formatting | bytes 114688 | tf_op args[6]
  3.8 138.2 %shard_map.94 = (f32[224,64]{1,0:T(8,128)}, f32[224,64]{1,0:T(8,128)}, f32[224,64]{1,0:T(8,128)}) custom-call(bf16[448,7168]{1,0:T(8,128)(2,1)} %acts.1, bf16[448,512]{1,0:T(8,128)(2,1)} %upstream.1, bf16[224,512]{1,0:T(8,128)(2,1)} %k_weight.1, bf16[224,512]{1,0:T(8,128)(2,1)} %probe.1, f32[1,128]{1,0:T(1,128)} %bitcast.1, f32[224,64]{1,0:T(8,128)} %copy.10.momentum, ...), custom_call_target="tpu_custom_call" | custom-call | tf_op jit(solution)/shard_map/pallas_call | solution.py:457
  142.0 1.6 %copy.12 = f32[224,64]{0,1:T(8,128)} copy(f32[224,64]{1,0:T(8,128)} %get-tuple-element.3) | data formatting | bytes 114688 | tf_op jit(solution)/shard_map/pallas_call | solution.py:457
  143.6 1.6 %copy.13 = f32[224,64]{0,1:T(8,128)} copy(f32[224,64]{1,0:T(8,128)} %get-tuple-element.4) | data formatting | bytes 114688 | tf_op jit(solution)/shard_map/pallas_call | solution.py:457
  145.2 1.6 %copy.14 = f32[224,64]{0,1:T(8,128)} copy(f32[224,64]{1,0:T(8,128)} %get-tuple-element.5) | data formatting | bytes 114688 | tf_op jit(solution)/shard_map/pallas_call | solution.py:457

commit v2 on v1

--- a/solution.py
+++ b/solution.py
@@ -9,14 +9,14 @@
 F32 = jnp.float32
 BF16 = jnp.bfloat16
 TOK = 448
+ROWS_A, ROWS_B, ROWS_C = 80, 96, 48
 D = 7168
 NX = 400
 
 
-def kernel(acts, upstream, k_weight, probe, gain, momentum, curvature,
-           out_m, out_c, out_u,
+def kernel(acts, upstream, k_weight, probe, gain, out,
            wp, av, at, acc, upv, gs, csend, crecv, rsend, rech, recf, s_buf,
-           yrecv, t_buf, zrecv, mom_v, cur_v, send_sems, recv_sems, loc_sems):
+           yrecv, t_buf, zrecv, send_sems, recv_sems, loc_sems):
     dp = lax.axis_index("dp")
     fs = lax.axis_index("fsdp")
     y, zl = dp // 2, lax.rem(dp, 2)
@@ -46,23 +46,33 @@
         cp.start()
         return cp
 
-    low_rows, high_rows = pl.ds(0, 112), pl.ds(112, 112)
-    quarter = wp.at[zh, x, c, high_rows, pl.ds(pl.multiple_of(y * 256, 256), 256)]
+    lo, hi, ends = pl.ds(0, ROWS_A), pl.ds(ROWS_A, ROWS_B), pl.ds(ROWS_A + ROWS_B, ROWS_C)
+    quarter = wp.at[zh, x, c, hi, pl.ds(pl.multiple_of(y * 256, 256), 256)]
     part_cols = pl.ds(pl.multiple_of(lax.rem(y, 2) * 256, 256), 256)
+    side = wp.at[zh, x, c, ends, pl.ds(pl.multiple_of(zl * 512, 512), 512)]
 
     @pl.when(y < 2)
     def _():
-        pltpu.make_async_copy(k_weight.at[high_rows, part_cols], quarter, loc_sems.at[13]).start()
+        pltpu.make_async_copy(k_weight.at[hi, part_cols], quarter, loc_sems.at[13]).start()
 
     @pl.when(y >= 2)
     def _():
-        pltpu.make_async_copy(probe.at[high_rows, part_cols], quarter, loc_sems.at[13]).start()
-
-    own = [local(k_weight.at[low_rows], wp.at[zh, x, c, low_rows, pl.ds(0, 512)], 0),
-           local(probe.at[low_rows], wp.at[zh, x, c, low_rows, pl.ds(512, 512)], 1),
-           pltpu.make_async_copy(k_weight.at[high_rows, part_cols], quarter, loc_sems.at[13])]
+        pltpu.make_async_copy(probe.at[hi, part_cols], quarter, loc_sems.at[13]).start()
+
+    @pl.when(zl == 0)
+    def _():
+        pltpu.make_async_copy(k_weight.at[ends], side, loc_sems.at[14]).start()
+
+    @pl.when(zl == 1)
+    def _():
+        pltpu.make_async_copy(probe.at[ends], side, loc_sems.at[14]).start()
+
+    own = [local(k_weight.at[lo], wp.at[zh, x, c, lo, pl.ds(0, 512)], 0),
+           local(probe.at[lo], wp.at[zh, x, c, lo, pl.ds(512, 512)], 1),
+           pltpu.make_async_copy(k_weight.at[hi, part_cols], quarter, loc_sems.at[13]),
+           pltpu.make_async_copy(k_weight.at[ends], side, loc_sems.at[14])]
     acp = [local(acts.at[:, pl.ds(i * 896, 896)], av.at[:, pl.ds(i * 896, 896)], 2 + i) for i in range(8)]
-    misc = [local(upstream, upv, 10), local(momentum, mom_v, 11), local(curvature, cur_v, 12)]
+    misc = [local(upstream, upv, 10)]
 
     for p in peers:
         pl.semaphore_signal(barrier, inc=1, device_id=p, device_id_type=MESH)
@@ -108,7 +118,27 @@
             self.hp.wait_recv()
             self.hm.wait_recv()
 
-    lo, hi = pl.ds(0, 112), pl.ds(112, 112)
+    class Ring8:
+        def __init__(self, xq):
+            self.xq = xq
+
+        def block(self, zz, off=0, width=512):
+            col = pl.multiple_of(lax.rem(zz, 2) * 512 + off, 128)
+            return wp.at[zz // 2, self.xq, c, ends, pl.ds(col, width)]
+
+        def hop(self, n):
+            if n > 1:
+                self.p.wait_recv()
+                self.m.wait_recv()
+            if n == 5:
+                return
+            low, high = lax.rem(z - n + 9, 8), lax.rem(z + n - 1, 8)
+            width = 512 if n < 4 else 256
+            r = self.block(low, 0, width)
+            self.p = xfer(r, r, dev_z(lax.rem(z + 1, 8)))
+            r = self.block(high, 512 - width, width)
+            self.m = xfer(r, r, dev_z(lax.rem(z + 7, 8)))
+
     yc = pl.multiple_of(y * 256, 256)
 
     def bz_half(q, i):
@@ -117,6 +147,11 @@
     bz = Ring(lambda q: wp.at[q, x, c, hi, pl.ds(yc, 256)], bz_half, zh, dev(dz=1), dev(dz=-1))
     az = Ring(lambda q: wp.at[q, x, c, lo, :],
               lambda q, i: wp.at[q, x, c, lo, pl.ds(i * 512, 512)], zh, dev(dz=1), dev(dz=-1))
+    zc = pl.multiple_of(zl * 512, 512)
+    cx = Ring(lambda q: wp.at[zh, q, c, ends, pl.ds(zc, 512)],
+              lambda q, i: wp.at[zh, q, c, ends, pl.ds(pl.multiple_of(zc + i * 256, 256), 256)],
+              x, dev(dx=1), dev(dx=-1))
+    cz = {dx: Ring8(m4(x + dx)) for dx in (0, -1, 1, 2)}
     bx, ax, by = {}, {}, {}
     for dz in (0, -1, 1, 2):
         def mk(q):
@@ -134,7 +169,7 @@
     core = {}
 
     def core_send(kind, dz):
-        r = wp.at[m4(zh + dz), :, c, lo if kind == "a" else hi, :]
+        r = wp.at[m4(zh + dz), :, c, {"a": lo, "b": hi, "c": ends}[kind], :]
         core[kind, dz] = xfer(r, r, partner)
 
     def transpose(i):
@@ -153,6 +188,7 @@
     def forward(dz):
         core["a", dz].wait_recv()
         core["b", dz].wait_recv()
+        core["c", dz].wait_recv()
         q = m4(zh + dz)
         init = first[0]
         first[0] = False
@@ -167,70 +203,97 @@
 
     for cp in own:
         cp.wait()
+    bx[0].start()
     bz.start()
-    bx[0].start()
+    az.start()
+    transpose(0)
     ax[0].start()
-    transpose(0)
     bx[0].mid()
     bz.mid()
-    az.start()
+    cx.start()
     bx[-1].start()
-    bx[1].start()
-    transpose(1)
     bx[0].end()
     by[0].start()
+    bx[1].start()
+    cx.mid()
+    cz[1].hop(1)
+    bx[-1].mid()
+    ax[0].mid()
+    transpose(1)
+    cz[0].hop(1)
+    bx[1].mid()
+    bx[-1].end()
+    by[-1].start()
+    az.mid()
+    cx.end()
+    ax[-1].start()
+    cz[2].hop(1)
     transpose(2)
-    bx[-1].mid()
-    bx[1].mid()
-    ax[0].mid()
+    cz[1].hop(2)
     bz.end()
     bx[2].start()
+    ax[0].end()
+    by[0].mid()
     transpose(3)
-    bx[-1].end()
-    by[-1].start()
-    bx[1].end()
-    by[1].start()
+    ax[-1].mid()
+    by[-1].mid()
+    cz[-1].hop(1)
     transpose(4)
     bx[2].mid()
+    cz[0].hop(2)
+    ax[1].start()
+    az.end()
+    bx[1].end()
+    cz[1].hop(3)
+    core_send("a", 0)
+    by[0].end()
+    by[1].start()
+    ax[2].start()
+    cz[-1].hop(2)
+    core_send("b", 0)
+    ax[-1].end()
     transpose(5)
+    cz[2].hop(2)
+    cz[0].hop(3)
+    by[-1].end()
+    core_send("c", 0)
+    transpose(6)
     bx[2].end()
+    core_send("b", -1)
+    cz[-1].hop(3)
+    core_send("a", -1)
     by[2].start()
-    by[0].mid()
-    ax[0].end()
-    core_send("a", 0)
-    transpose(6)
-    az.mid()
-    ax[-1].start()
-    ax[1].start()
+    ax[1].mid()
+    cz[2].hop(3)
+    cz[-1].hop(4)
+    cz[1].hop(4)
     transpose(7)
-    by[0].end()
-    core_send("b", 0)
-    by[-1].mid()
+    cz[2].hop(4)
+    cz[0].hop(4)
+    core_send("c", -1)
+    by[1].mid()
+    core_send("c", 1)
+    ax[2].mid()
     forward(0)
-    az.end()
-    ax[2].start()
-    by[-1].end()
-    core_send("b", -1)
-    ax[-1].mid()
-    ax[1].mid()
-    by[1].mid()
-    ax[-1].end()
-    core_send("a", -1)
+    by[2].mid()
+    ax[1].end()
+    core_send("a", 1)
+    cz[2].hop(5)
+    cz[-1].hop(5)
+    cz[0].hop(5)
+    cz[1].hop(5)
     by[1].end()
     core_send("b", 1)
+    ax[2].end()
+    core_send("c", 2)
+    core_send("a", 2)
     forward(-1)
-    ax[1].end()
-    core_send("a", 1)
-    by[2].mid()
-    ax[2].mid()
-    forward(1)
     by[2].end()
     core_send("b", 2)
-    ax[2].end()
-    core_send("a", 2)
+    forward(1)
+    forward(2)
     for cp in misc:
         cp.wait()
-    forward(2)
 
     RB = 64
 
@@ -417,6 +480,7 @@
     for k in range(2):
         chunk_z(k, zorder[-1])
 
+    sums = []
     own_rows = pl.ds(pl.multiple_of(zh * 112, 16), 112)
     for k in range(2):
         for d in range(1, 8):
@@ -426,17 +490,12 @@
         total = t_buf[k, own_rows, pl.ds(pl.multiple_of(zl * 128, 128), 128)].astype(F32)
         for d in range(1, 8):
             total = total + zrecv[k, d].astype(F32)
-        rk = pl.ds(k * 112, 112)
-        g = total[:, :64]
-        hv = pltpu.roll(total, 64, axis=1)[:, :64]
-        pc = wp[zh, x, c, rk, pl.ds(pl.multiple_of(512 + y * 128, 128), 128)].astype(F32)
-        pcr = pltpu.roll(pc, 64, axis=1)
-        pv = jnp.where(zl == 0, pc, pcr)[:, :64]
-        nm = 0.965 * mom_v[rk, :] + 0.035 * g
-        nc = 0.99 * cur_v[rk, :] + 0.01 * (pv * hv)
-        out_m[rk, :] = nm
-        out_c[rk, :] = nc
-        out_u[rk, :] = jnp.clip(nm / jnp.maximum(0.5 * nc, 0.25), -1.0, 1.0)
+        sums.append(total)
+    total = jnp.concatenate(sums, axis=0).T
+    head_cols = pl.ds(pl.multiple_of(512 + y * 128, 128), 128)
+    probe_t = wp[zh, x, c, :, head_cols].astype(F32).T
+    out[pl.ds(0, 64), :] = total[:64]
+    out[pl.ds(64, 64), :] = total[64:] * jnp.where(zl == 0, probe_t[:64], probe_t[64:])
 
     for cp in sent:
         cp.wait_send()
@@ -453,12 +512,11 @@
 def on_device(acts, upstream, k_weight, probe, norm_gain, momentum, curvature):
     any_spec = pl.BlockSpec(memory_space=pl.ANY)
     vmem = pl.BlockSpec(memory_space=pltpu.VMEM)
-    out = jax.ShapeDtypeStruct((224, 64), F32)
-    return pl.pallas_call(
+    sums = pl.pallas_call(
         kernel,
-        out_shape=(out, out, out),
-        in_specs=[any_spec] * 4 + [vmem] + [any_spec] * 2,
-        out_specs=(vmem, vmem, vmem),
+        out_shape=jax.ShapeDtypeStruct((128, 224), F32),
+        in_specs=[any_spec] * 4 + [vmem],
+        out_specs=vmem,
         scratch_shapes=[
             pltpu.VMEM((4, 4, 2, 224, 1024), BF16),
             pltpu.VMEM((TOK, D), BF16),
@@ -475,15 +533,17 @@
             pltpu.VMEM((2, 3, 448, 256), BF16),
             pltpu.VMEM((2, 448, 256), BF16),
             pltpu.VMEM((2, 8, 112, 128), BF16),
-            pltpu.VMEM((224, 64), F32),
-            pltpu.VMEM((224, 64), F32),
             pltpu.SemaphoreType.DMA((NX,)),
             pltpu.SemaphoreType.DMA((NX,)),
             pltpu.SemaphoreType.DMA((16,)),
         ],
         compiler_params=pltpu.CompilerParams(
             collective_id=0, has_side_effects=True, vmem_limit_bytes=67043328),
-    )(acts, upstream, k_weight, probe, norm_gain.reshape(1, 128), momentum, curvature)
+    )(acts, upstream, k_weight, probe, norm_gain.reshape(1, 128))
+    new_momentum = 0.965 * momentum.T + 0.035 * sums[:64]
+    new_curvature = 0.99 * curvature.T + 0.01 * sums[64:]
+    update = jnp.clip(new_momentum / jnp.maximum(0.5 * new_curvature, 0.25), -1.0, 1.0)
+    return (new_momentum.T, new_curvature.T, update.T)
 
 
 def solution(mesh):

time: 147 us -> 125 us (0.85)
  Pallas kernels: 138 us -> 123 us
  local copies, waits for them, and re-layouts: 7.98 us -> 0 us
  other arithmetic: 0 us -> 1.62 us
    pallas_call x1, Pallas kernels: 138 us -> 123 us  [on_device(): pl.pallas_call(kernel, out_shape=jax.ShapeDtypeStruct((128, 224), F32), i...]
    pallas_call x3 -> x0, local copies, waits for them, and re-layouts: 4.83 us -> none  [on_device(): pl.pallas_call(kernel, out_shape=(out, out, out), in_specs=[any_spec] * 4...]
    unnamed x2 -> x0, local copies, waits for them, and re-layouts: 3.15 us -> none
    transpose x0 -> x1, other arithmetic: none -> 1.62 us  [on_device(): return (new_momentum.T, new_curvature.T, update.T)]
where the time goes in v2:
time: 125 us
  Pallas kernels  123 us (98%)
  other arithmetic  1.62 us (1%)
    pallas_call x1, Pallas kernels, on_device(): pl.pallas_call(kernel, out_shape=jax.ShapeDtypeStruct((128, 224), F32), i...  123 us

profile of v2, /device:TPU:8, one launch (start us, length us, event | category | flops | bytes accessed | tf_op | source)
XLA Modules:
  0.0 125.1 jit_solution(6574164550902015018)
XLA Ops:
  0.6 122.8 %shard_map.94 = f32[128,224]{1,0:T(8,128)} custom-call(bf16[448,7168]{1,0:T(8,128)(2,1)} %acts.1, bf16[448,512]{1,0:T(8,128)(2,1)} %upstream.1, bf16[224,512]{1,0:T(8,128)(2,1)} %k_weight.1, bf16[224,512]{1,0:T(8,128)(2,1)} %probe.1, f32[1,128]{1,0:T(1,128)} %bitcast.19), custom_call_target="tpu_custom_call" | custom-call | tf_op jit(solution)/shard_map/pallas_call | solution.py:515
  123.5 1.6 %clamp_bitcast_fusion = (f32[224,64]{0,1:T(8,128)}, f32[224,64]{0,1:T(8,128)}, f32[224,64]{0,1:T(8,128)}) fusion(f32[128,224]{1,0:T(8,128)} %shard_map.94, f32[224,64]{0,1:T(8,128)} %param.12, f32[224,64]{0,1:T(8,128)} %param.13), kind=kLoop, calls=%fused_computation.2 | loop fusion | flops 143360 | bytes 401408 | tf_op jit(solution)/shard_map/transpose | solution.py:546

commit v3 on v2

--- a/solution.py
+++ b/solution.py
@@ -9,6 +9,8 @@
 F32 = jnp.float32
 BF16 = jnp.bfloat16
 TOK = 448
+RA = 80
+RC = 224 - 2 * RA
 ROWS_A, ROWS_B, ROWS_C = 80, 96, 48
 D = 7168
 NX = 400
@@ -16,7 +18,8 @@
 
 def kernel(acts, upstream, k_weight, probe, gain, out,
            wp, av, at, acc, upv, gs, csend, crecv, rsend, rech, recf, s_buf,
-           yrecv, t_buf, zrecv, send_sems, recv_sems, loc_sems):
+           far2, near2, t_buf, zrecv,
+           at_z, zsend, zcrecv, o_buf, zfar, znear, xrecv, u_buf, y3recv, send_sems, recv_sems, loc_sems):
     dp = lax.axis_index("dp")
     fs = lax.axis_index("fsdp")
     y, zl = dp // 2, lax.rem(dp, 2)
@@ -179,9 +182,10 @@
         tr = blk.T
         for xx in range(2):
             for cc in range(2):
+                r0 = xx * 448 + cc * 224
                 for col in range(2):
-                    r0 = xx * 448 + cc * 224 + col * 112
-                    at[col, xp * 2 + xx, cc, pl.ds(q * 112, 112), :] = tr[r0:r0 + 112, :]
+                    at[col, xp * 2 + xx, cc, pl.ds(q * RA, RA), :] = tr[r0 + col * RA:r0 + (col + 1) * RA, :]
+                at_z[q, cc, pl.ds((xp * 2 + xx) * RC, RC), :] = tr[r0 + 2 * RA:r0 + 224, :]
 
     first = [True]
 
@@ -336,14 +340,19 @@
         xi, yj = (uq, v) if k == 0 else (v, uq)
         return jnp.dot(at[k, xi, cc], gs[yj], preferred_element_type=F32)
 
-    ds_order = (2, 1, -1, 0)
+    def rows_of(dz):
+        return pl.ds(pl.multiple_of(m4(zh + dz) * RA, 16), RA)
+
+    step_of = {2: 0, 1: 1, -1: 2, 0: 3}
     core_rs = {}
 
-    def part_p(k, i):
+    def part_p(k, d):
+        i = step_of[d]
         if i >= 2:
-            core_rs[k, i - 2].wait_send()
-            sent[:] = [cp for cp in sent if cp is not core_rs[k, i - 2]]
-        uq = m4(u[k] + ds_order[i])
+            old = core_rs[k, i - 2]
+            old.wait_send()
+            sent[:] = [cp for cp in sent if cp is not old]
+        uq = m4(u[k] + d)
 
         def body(v, carry):
             csend[k, i % 2, v] = tile(k, uq, v, 1 - c).astype(BF16)
@@ -352,30 +361,25 @@
         lax.fori_loop(0, 4, body, 0)
         core_rs[k, i] = xfer(csend.at[k, i % 2], crecv.at[k, i], partner)
 
-    half_base = {}
-
-    def half_copy(k, v):
-        device = udev(k, 1 - 2 * (v // 2))
-        return rdma(rsend.at[k, 0, v], rech.at[k, v], device, half_base[k] + v)
-
-    def part_far(k):
+    halves = {}
+
+    def far(k):
         core_rs[k, 0].wait_recv()
-        half_base[k] = take(4)
         uq = m4(u[k] + 2)
 
         def body(v, carry):
             rsend[k, 0, v] = (tile(k, uq, v, c) + crecv[k, 0, v].astype(F32)).astype(BF16)
-            half_copy(k, v).start()
             return carry
 
-        lax.fori_loop(0, 4, body, 0)
+        for p in range(2):
+            lax.fori_loop(2 * p, 2 * p + 2, body, 0)
+            halves[k, p] = xfer(rsend.at[k, 0, pl.ds(2 * p, 2)], rech.at[k, pl.ds(2 * p, 2)], udev(k, 1 - 2 * p))
 
     early, late = {}, {}
-    zorder = (2, 1, -1, 0)
-
-    def near_free(k, i):
+
+    def near_free(k, d):
+        i = step_of[d]
         core_rs[k, i].wait_recv()
-        d = ds_order[i]
         uq = m4(u[k] + d)
         v0 = 2 if d == 1 else 0
 
@@ -386,20 +390,19 @@
         lax.fori_loop(v0, v0 + 2, body, 0)
         early[k, i] = xfer(rsend.at[k, i, pl.ds(v0, 2)], recf.at[k, i - 1, pl.ds(v0, 2)], udev(k, d))
 
-    def near_sum(k, i):
-        d = ds_order[i]
+    def near_sum(k, d):
+        i = step_of[d]
         uq = m4(u[k] + d)
         v0 = 0 if d == 1 else 2
-        half_copy(k, v0).wait_recv()
-        half_copy(k, v0 + 1).wait_recv()
+        halves[k, v0 // 2].wait_recv()
 
         def body(v, carry):
             rsend[k, i, v] = (tile(k, uq, v, c) + crecv[k, i, v].astype(F32) + rech[k, v].astype(F32)).astype(BF16)
             return carry
 
         lax.fori_loop(v0, v0 + 2, body, 0)
-        for dz in zorder:
-            rows = pl.ds(pl.multiple_of(m4(zh + dz) * 112, 16), 112)
+        for dz in (2, 1, -1, 0):
+            rows = rows_of(dz)
             late[k, i, dz] = xfer(rsend.at[k, i, pl.ds(v0, 2), rows], recf.at[k, i - 1, pl.ds(v0, 2), rows], udev(k, d))
 
     def part_own(k):
@@ -411,13 +414,15 @@
 
         lax.fori_loop(0, 4, body, 0)
 
-    phase2 = {}
+    second = {}
+    seen = set()
 
     def chunk_sum(k, dz):
-        rows = pl.ds(pl.multiple_of(m4(zh + dz) * 112, 16), 112)
+        rows = rows_of(dz)
         for i in (1, 2):
-            if dz == zorder[0]:
+            if (k, i) not in seen:
                 early[k, i].wait_recv()
+                seen.add((k, i))
             late[k, i, dz].wait_recv()
 
         def body(v, carry):
@@ -426,9 +431,18 @@
             return carry
 
         lax.fori_loop(0, 4, body, 0)
-        for d in (2, 1, 3):
-            vq = m4(v_own[k] + d)
-            phase2[k, dz, d] = xfer(s_buf.at[k, vq, rows], yrecv.at[k, d - 1, rows], vdev(k, d))
+        vq = m4(v_own[k] + 2)
+        for p in range(2):
+            second[k, dz, p] = xfer(s_buf.at[k, vq, rows, pl.ds(128 * p, 128)], far2.at[k, p, rows], vdev(k, 1 - 2 * p))
+
+    def chunk_mid(k, dz):
+        rows = rows_of(dz)
+        for p in range(2):
+            second[k, dz, p].wait_recv()
+            vq = m4(v_own[k] + 1 - 2 * p)
+            cols = pl.ds(128 * p, 128)
+            s_buf[k, vq, rows, cols] = (s_buf[k, vq, rows, cols].astype(F32) + far2[k, p, rows].astype(F32)).astype(BF16)
+            second[k, dz, 2 + p] = xfer(s_buf.at[k, vq, rows], near2.at[k, p, rows], vdev(k, 1 - 2 * p))
 
     zbase = (take(8), take(8))
 
@@ -439,49 +453,166 @@
 
     def chunk_z(k, dz):
         q = m4(zh + dz)
-        rows = pl.ds(pl.multiple_of(q * 112, 16), 112)
-        for d in (1, 2, 3):
-            phase2[k, dz, d].wait_recv()
-        total = s_buf[k, v_own[k], rows].astype(F32)
-        for d in range(3):
-            total = total + yrecv[k, d, rows].astype(F32)
-        t_buf[k, rows] = total.astype(BF16)
+        rows = rows_of(dz)
+        second[k, dz, 2].wait_recv()
+        second[k, dz, 3].wait_recv()
+        t_buf[k, rows] = (s_buf[k, v_own[k], rows].astype(F32) + near2[k, 0, rows].astype(F32)
+                          + near2[k, 1, rows].astype(F32)).astype(BF16)
         if dz == 0:
             z_copy(k, rows, 2 * zh + (1 - zl), 1 - zl).start()
         else:
             for l in range(2):
                 z_copy(k, rows, 2 * q + l, jnp.int32(l)).start()
 
+    core_z = {}
+
+    def part_pz(dz):
+        q = m4(zh + dz)
+
+        def body(j, carry):
+            zsend[q, j] = jnp.dot(at_z[q, 1 - c], gs[j], preferred_element_type=F32).astype(BF16)
+            return carry
+
+        lax.fori_loop(0, 4, body, 0)
+        core_z[dz] = xfer(zsend.at[q], zcrecv.at[q], partner)
+
+    def part_oz(dz):
+        q = m4(zh + dz)
+        core_z[dz].wait_recv()
+
+        def body(j, carry):
+            o_buf[q, j] = (jnp.dot(at_z[q, c], gs[j], preferred_element_type=F32) + zcrecv[q, j].astype(F32)).astype(BF16)
+            return carry
+
+        lax.fori_loop(0, 4, body, 0)
+
+    chain = {}
+    up, down = dev_z(lax.rem(z + 1, 8)), dev_z(lax.rem(z + 7, 8))
+
+    def z_block(zz):
+        return zz // 2, pl.ds(pl.multiple_of(lax.rem(zz, 2) * 128, 128), 128)
+
+    def add_z(zz, j, value):
+        q, cols = z_block(zz)
+        o_buf[q, j, :, cols] = (o_buf[q, j, :, cols].astype(F32) + value.astype(F32)).astype(BF16)
+
+    def z_far():
+        q, cols = z_block(lax.rem(z + 4, 8))
+        for p, device in ((0, up), (1, down)):
+            chain[4, p, p] = xfer(o_buf.at[q, pl.ds(2 * p, 2), :, cols], zfar.at[p], device)
+
+    def z_step(n, h):
+        for p, device in ((0, up), (1, down)):
+            zz = lax.rem(z + 8 + (n if p == 0 else -n), 8)
+            q, cols = z_block(zz)
+            if n == 3:
+                if h == p:
+                    chain[4, p, p].wait_recv()
+                    for j in range(2):
+                        add_z(zz, 2 * p + j, zfar[p, j])
+            else:
+                chain[n + 1, p, h].wait_recv()
+                for j in range(2):
+                    add_z(zz, 2 * h + j, znear[p, 2 - n, 2 * h + j])
+            chain[n, p, h] = xfer(o_buf.at[q, pl.ds(2 * h, 2), :, cols],
+                                  znear.at[p, 3 - n, pl.ds(2 * h, 2)], device)
+
+    def z_own(h):
+        q, cols = z_block(z)
+        for p in range(2):
+            chain[1, p, h].wait_recv()
+        for j in range(2 * h, 2 * h + 2):
+            o_buf[q, j, :, cols] = (o_buf[q, j, :, cols].astype(F32) + znear[0, 2, j].astype(F32)
+                                    + znear[1, 2, j].astype(F32)).astype(BF16)
+        for d in (2, 1, 3):
+            xq = m4(x + d)
+            chain["x", d, h] = xfer(o_buf.at[q, pl.ds(2 * h, 2), pl.ds(pl.multiple_of(xq * RC, 16), RC), cols],
+                                    xrecv.at[d - 1, pl.ds(2 * h, 2)], dev(dx=d))
+
+    def z_x():
+        q, cols = z_block(z)
+        for d in (1, 2, 3):
+            for h in range(2):
+                chain["x", d, h].wait_recv()
+        own_x = pl.ds(pl.multiple_of(x * RC, 16), RC)
+        for j in range(4):
+            total = o_buf[q, j, own_x, cols].astype(F32)
+            for d in range(3):
+                total = total + xrecv[d, j].astype(F32)
+            u_buf[j] = total.astype(BF16)
+        for d in (2, 1, 3):
+            chain["y", d] = xfer(u_buf.at[m4(y + d)], y3recv.at[d - 1], dev(dy=d))
+
+    part_p(0, 2)
+    part_p(1, 2)
+    part_p(1, 1)
+    part_pz(2)
+    far(0)
+    far(1)
+    part_p(0, 1)
+    part_p(1, -1)
+    near_free(1, 1)
+    part_oz(2)
+    z_far()
+    near_free(0, 1)
+    part_p(0, -1)
+    part_pz(-1)
+    part_pz(1)
+    part_p(1, 0)
+    near_free(1, -1)
+    near_free(0, -1)
+    part_oz(-1)
+    part_oz(1)
+    z_step(3, 1)
+    part_pz(0)
+    z_step(3, 0)
+    near_sum(1, 1)
+    near_sum(0, -1)
+    near_sum(0, 1)
+    z_step(2, 1)
+    near_sum(1, -1)
     part_p(0, 0)
-    part_p(1, 0)
-    part_far(0)
-    part_far(1)
-    part_p(0, 1)
-    part_p(0, 2)
-    part_p(1, 1)
-    part_p(1, 2)
-    near_free(0, 1)
-    near_free(0, 2)
-    near_free(1, 1)
-    near_free(1, 2)
-    part_p(0, 3)
-    part_p(1, 3)
-    near_sum(0, 1)
-    near_sum(0, 2)
-    near_sum(1, 1)
-    near_sum(1, 2)
+    part_own(1)
+    part_oz(0)
+    z_step(2, 0)
     part_own(0)
-    part_own(1)
-    for j, dz in enumerate(zorder):
-        for k in range(2):
-            chunk_sum(k, dz)
-            if j:
-                chunk_z(k, zorder[j - 1])
-    for k in range(2):
-        chunk_z(k, zorder[-1])
+    z_step(1, 1)
+    chunk_sum(1, 1)
+    chunk_sum(1, 2)
+    chunk_sum(0, 1)
+    chunk_sum(1, -1)
+    z_step(1, 0)
+    chunk_mid(1, 1)
+    chunk_sum(0, 2)
+    chunk_mid(1, 2)
+    chunk_sum(0, 0)
+    chunk_mid(0, 1)
+    chunk_sum(0, -1)
+    chunk_mid(1, -1)
+    chunk_mid(0, 2)
+    chunk_sum(1, 0)
+    chunk_z(1, 1)
+    z_own(1)
+    chunk_z(0, 1)
+    z_own(0)
+    chunk_mid(0, -1)
+    chunk_z(1, 2)
+    chunk_mid(1, 0)
+    chunk_mid(0, 0)
+    chunk_z(0, 2)
+    chunk_z(0, -1)
+    chunk_z(0, 0)
+    chunk_z(1, -1)
+    z_x()
+    chunk_z(1, 0)
 
     sums = []
-    own_rows = pl.ds(pl.multiple_of(zh * 112, 16), 112)
+    own_rows = pl.ds(pl.multiple_of(zh * RA, 16), RA)
+    for d in (1, 2, 3):
+        chain["y", d].wait_recv()
+    last = u_buf[y].astype(F32)
+    for d in range(3):
+        last = last + y3recv[d].astype(F32)
     for k in range(2):
         for d in range(1, 8):
             pltpu.make_async_remote_copy(
@@ -491,7 +622,7 @@
         for d in range(1, 8):
             total = total + zrecv[k, d].astype(F32)
         sums.append(total)
-    total = jnp.concatenate(sums, axis=0).T
+    total = jnp.concatenate(sums + [last], axis=0).T
     head_cols = pl.ds(pl.multiple_of(512 + y * 128, 128), 128)
     probe_t = wp[zh, x, c, :, head_cols].astype(F32).T
     out[pl.ds(0, 64), :] = total[:64]
@@ -500,8 +631,6 @@
     for cp in sent:
         cp.wait_send()
     for k in range(2):
-        for v in range(4):
-            half_copy(k, v).wait_send()
         for d in range(1, 8):
             pltpu.make_async_remote_copy(
                 src_ref=zrecv.at[k, 0], dst_ref=zrecv.at[k, d], send_sem=send_sems.at[zbase[k] + d],
@@ -520,19 +649,29 @@
         scratch_shapes=[
             pltpu.VMEM((4, 4, 2, 224, 1024), BF16),
             pltpu.VMEM((TOK, D), BF16),
-            pltpu.VMEM((2, 4, 2, 448, 448), BF16),
+            pltpu.VMEM((2, 4, 2, 4 * RA, TOK), BF16),
             pltpu.VMEM((TOK, 1024), F32),
             pltpu.VMEM((TOK, 512), BF16),
             pltpu.VMEM((4, TOK, 256), BF16),
-            pltpu.VMEM((2, 2, 4, 448, 256), BF16),
-            pltpu.VMEM((2, 4, 4, 448, 256), BF16),
-            pltpu.VMEM((2, 3, 4, 448, 256), BF16),
-            pltpu.VMEM((2, 4, 448, 256), BF16),
-            pltpu.VMEM((2, 2, 4, 448, 256), BF16),
-            pltpu.VMEM((2, 4, 448, 256), BF16),
-            pltpu.VMEM((2, 3, 448, 256), BF16),
-            pltpu.VMEM((2, 448, 256), BF16),
-            pltpu.VMEM((2, 8, 112, 128), BF16),
+            pltpu.VMEM((2, 2, 4, 4 * RA, 256), BF16),
+            pltpu.VMEM((2, 4, 4, 4 * RA, 256), BF16),
+            pltpu.VMEM((2, 3, 4, 4 * RA, 256), BF16),
+            pltpu.VMEM((2, 4, 4 * RA, 256), BF16),
+            pltpu.VMEM((2, 2, 4, 4 * RA, 256), BF16),
+            pltpu.VMEM((2, 4, 4 * RA, 256), BF16),
+            pltpu.VMEM((2, 2, 4 * RA, 128), BF16),
+            pltpu.VMEM((2, 2, 4 * RA, 256), BF16),
+            pltpu.VMEM((2, 4 * RA, 256), BF16),
+            pltpu.VMEM((2, 8, RA, 128), BF16),
+            pltpu.VMEM((4, 2, 4 * RC, TOK), BF16),
+            pltpu.VMEM((4, 4, 4 * RC, 256), BF16),
+            pltpu.VMEM((4, 4, 4 * RC, 256), BF16),
+            pltpu.VMEM((4, 4, 4 * RC, 256), BF16),
+            pltpu.VMEM((2, 2, 4 * RC, 128), BF16),
+            pltpu.VMEM((2, 3, 4, 4 * RC, 128), BF16),
+            pltpu.VMEM((3, 4, RC, 128), BF16),
+            pltpu.VMEM((4, RC, 128), BF16),
+            pltpu.VMEM((3, RC, 128), BF16),
             pltpu.SemaphoreType.DMA((NX,)),
             pltpu.SemaphoreType.DMA((NX,)),
             pltpu.SemaphoreType.DMA((16,)),

time: 125 us -> 119 us (0.952)
  Pallas kernels: 123 us -> 116 us
    pallas_call x1, Pallas kernels: 123 us -> 116 us  [on_device(): pl.pallas_call(kernel, out_shape=jax.ShapeDtypeStruct((128, 224), F32), i...]
where the time goes in v3:
time: 119 us
  Pallas kernels  116 us (97%)
  other arithmetic  1.62 us (1%)
    pallas_call x1, Pallas kernels, on_device(): pl.pallas_call(kernel, out_shape=jax.ShapeDtypeStruct((128, 224), F32), i...  116 us

profile of v3, /device:TPU:8, one launch (start us, length us, event | category | flops | bytes accessed | tf_op | source)
XLA Modules:
  0.0 118.5 jit_solution(14100114664778967649)
XLA Ops:
  0.6 116.3 %shard_map.94 = f32[128,224]{1,0:T(8,128)} custom-call(bf16[448,7168]{1,0:T(8,128)(2,1)} %acts.1, bf16[448,512]{1,0:T(8,128)(2,1)} %upstream.1, bf16[224,512]{1,0:T(8,128)(2,1)} %k_weight.1, bf16[224,512]{1,0:T(8,128)(2,1)} %probe.1, f32[1,128]{1,0:T(1,128)} %bitcast.19), custom_call_target="tpu_custom_call" | custom-call | tf_op jit(solution)/shard_map/pallas_call | solution.py:644
  116.9 1.6 %clamp_bitcast_fusion = (f32[224,64]{0,1:T(8,128)}, f32[224,64]{0,1:T(8,128)}, f32[224,64]{0,1:T(8,128)}) fusion(f32[128,224]{1,0:T(8,128)} %shard_map.94, f32[224,64]{0,1:T(8,128)} %param.12, f32[224,64]{0,1:T(8,128)} %param.13), kind=kLoop, calls=%fused_computation.2 | loop fusion | flops 143360 | bytes 401408 | tf_op jit(solution)/shard_map/transpose | solution.py:685

commit v4 on v3

--- a/solution.py
+++ b/solution.py
@@ -207,94 +207,94 @@
 
     for cp in own:
         cp.wait()
+    bz.start()
     bx[0].start()
-    bz.start()
+    ax[0].start()
+    transpose(0)
     az.start()
-    transpose(0)
-    ax[0].start()
     bx[0].mid()
     bz.mid()
+    bx[-1].start()
+    transpose(1)
     cx.start()
-    bx[-1].start()
+    bx[1].start()
     bx[0].end()
+    cz[0].hop(1)
     by[0].start()
-    bx[1].start()
+    bx[-1].mid()
     cx.mid()
+    ax[0].mid()
+    cz[-1].hop(1)
     cz[1].hop(1)
-    bx[-1].mid()
-    ax[0].mid()
-    transpose(1)
-    cz[0].hop(1)
-    bx[1].mid()
     bx[-1].end()
     by[-1].start()
+    bx[1].mid()
     az.mid()
+    ax[1].start()
+    transpose(2)
+    bz.end()
     cx.end()
+    cz[2].hop(1)
+    transpose(3)
+    bx[1].end()
+    ax[0].end()
+    bx[2].start()
+    by[1].start()
+    transpose(4)
+    cz[0].hop(2)
+    by[0].mid()
     ax[-1].start()
-    cz[2].hop(1)
-    transpose(2)
+    ax[1].mid()
     cz[1].hop(2)
-    bz.end()
-    bx[2].start()
-    ax[0].end()
-    by[0].mid()
-    transpose(3)
-    ax[-1].mid()
+    cz[-1].hop(2)
+    cz[2].hop(2)
     by[-1].mid()
-    cz[-1].hop(1)
-    transpose(4)
+    cz[0].hop(3)
+    by[1].mid()
     bx[2].mid()
-    cz[0].hop(2)
-    ax[1].start()
+    core_send("a", 0)
     az.end()
-    bx[1].end()
+    ax[2].start()
     cz[1].hop(3)
-    core_send("a", 0)
+    transpose(5)
+    cz[-1].hop(3)
+    ax[1].end()
+    cz[2].hop(3)
+    core_send("c", 0)
     by[0].end()
-    by[1].start()
-    ax[2].start()
-    cz[-1].hop(2)
-    core_send("b", 0)
-    ax[-1].end()
-    transpose(5)
-    cz[2].hop(2)
-    cz[0].hop(3)
-    by[-1].end()
-    core_send("c", 0)
     transpose(6)
     bx[2].end()
-    core_send("b", -1)
-    cz[-1].hop(3)
-    core_send("a", -1)
+    core_send("b", 0)
+    ax[-1].mid()
     by[2].start()
-    ax[1].mid()
-    cz[2].hop(3)
-    cz[-1].hop(4)
+    by[-1].end()
+    core_send("a", 1)
+    cz[0].hop(4)
     cz[1].hop(4)
     transpose(7)
+    core_send("b", -1)
+    cz[-1].hop(4)
+    ax[2].mid()
+    by[1].end()
+    core_send("b", 1)
     cz[2].hop(4)
-    cz[0].hop(4)
+    core_send("c", 1)
     core_send("c", -1)
-    by[1].mid()
-    core_send("c", 1)
-    ax[2].mid()
     forward(0)
     by[2].mid()
-    ax[1].end()
-    core_send("a", 1)
+    ax[2].end()
+    ax[-1].end()
+    cz[-1].hop(5)
+    core_send("a", -1)
+    cz[1].hop(5)
+    core_send("a", 2)
+    forward(1)
+    cz[0].hop(5)
     cz[2].hop(5)
-    cz[-1].hop(5)
-    cz[0].hop(5)
-    cz[1].hop(5)
-    by[1].end()
-    core_send("b", 1)
-    ax[2].end()
     core_send("c", 2)
-    core_send("a", 2)
-    forward(-1)
     by[2].end()
     core_send("b", 2)
-    forward(1)
+    forward(-1)
     forward(2)
     for cp in misc:
         cp.wait()
@@ -545,64 +545,64 @@
 
     part_p(0, 2)
     part_p(1, 2)
-    part_p(1, 1)
     part_pz(2)
+    part_p(0, 1)
     far(0)
     far(1)
-    part_p(0, 1)
-    part_p(1, -1)
-    near_free(1, 1)
+    part_p(1, 1)
     part_oz(2)
     z_far()
-    near_free(0, 1)
     part_p(0, -1)
     part_pz(-1)
+    part_p(1, -1)
     part_pz(1)
-    part_p(1, 0)
+    near_free(0, 1)
+    near_free(0, -1)
+    near_free(1, 1)
+    part_oz(-1)
     near_free(1, -1)
-    near_free(0, -1)
-    part_oz(-1)
     part_oz(1)
-    z_step(3, 1)
-    part_pz(0)
     z_step(3, 0)
     near_sum(1, 1)
+    z_step(3, 1)
     near_sum(0, -1)
     near_sum(0, 1)
+    part_p(1, 0)
+    near_sum(1, -1)
+    z_step(2, 0)
+    part_p(0, 0)
+    part_pz(0)
+    part_own(1)
     z_step(2, 1)
-    near_sum(1, -1)
-    part_p(0, 0)
-    part_own(1)
+    part_own(0)
     part_oz(0)
-    z_step(2, 0)
-    part_own(0)
+    chunk_sum(1, 2)
+    chunk_sum(0, 2)
+    z_step(1, 0)
+    chunk_sum(1, 1)
+    chunk_sum(1, -1)
     z_step(1, 1)
-    chunk_sum(1, 1)
-    chunk_sum(1, 2)
-    chunk_sum(0, 1)
-    chunk_sum(1, -1)
-    z_step(1, 0)
-    chunk_mid(1, 1)
-    chunk_sum(0, 2)
     chunk_mid(1, 2)
     chunk_sum(0, 0)
-    chunk_mid(0, 1)
+    chunk_mid(1, 1)
     chunk_sum(0, -1)
+    chunk_sum(1, 0)
+    chunk_sum(0, 1)
     chunk_mid(1, -1)
     chunk_mid(0, 2)
-    chunk_sum(1, 0)
+    z_own(0)
+    chunk_mid(0, 0)
+    chunk_z(1, 2)
+    chunk_mid(0, 1)
+    chunk_mid(0, -1)
     chunk_z(1, 1)
     z_own(1)
+    chunk_z(1, -1)
+    chunk_z(0, 2)
+    chunk_mid(1, 0)
+    chunk_z(0, 0)
     chunk_z(0, 1)
-    z_own(0)
-    chunk_mid(0, -1)
-    chunk_z(1, 2)
-    chunk_mid(1, 0)
-    chunk_mid(0, 0)
-    chunk_z(0, 2)
     chunk_z(0, -1)
-    chunk_z(0, 0)
-    chunk_z(1, -1)
     z_x()
     chunk_z(1, 0)
 

time: 119 us -> 112 us (0.941)
  Pallas kernels: 116 us -> 109 us
    pallas_call x1, Pallas kernels: 116 us -> 109 us  [on_device(): pl.pallas_call(kernel, out_shape=jax.ShapeDtypeStruct((128, 224), F32), i...]
where the time goes in v4:
time: 112 us
  Pallas kernels  109 us (97%)
  other arithmetic  1.62 us (1%)
    pallas_call x1, Pallas kernels, on_device(): pl.pallas_call(kernel, out_shape=jax.ShapeDtypeStruct((128, 224), F32), i...  109 us

profile of v4, /device:TPU:8, one launch (start us, length us, event | category | flops | bytes accessed | tf_op | source)
XLA Modules:
  0.0 111.5 jit_solution(9013094677529013878)
XLA Ops:
  0.6 109.3 %shard_map.94 = f32[128,224]{1,0:T(8,128)} custom-call(bf16[448,7168]{1,0:T(8,128)(2,1)} %acts.1, bf16[448,512]{1,0:T(8,128)(2,1)} %upstream.1, bf16[224,512]{1,0:T(8,128)(2,1)} %k_weight.1, bf16[224,512]{1,0:T(8,128)(2,1)} %probe.1, f32[1,128]{1,0:T(1,128)} %bitcast.19), custom_call_target="tpu_custom_call" | custom-call | tf_op jit(solution)/shard_map/pallas_call | solution.py:644
  109.9 1.6 %clamp_bitcast_fusion = (f32[224,64]{0,1:T(8,128)}, f32[224,64]{0,1:T(8,128)}, f32[224,64]{0,1:T(8,128)}) fusion(f32[128,224]{1,0:T(8,128)} %shard_map.94, f32[224,64]{0,1:T(8,128)} %param.12, f32[224,64]{0,1:T(8,128)} %param.13), kind=kLoop, calls=%fused_computation.2 | loop fusion | flops 143360 | bytes 401408 | tf_op jit(solution)/shard_map/transpose | solution.py:685
